TPU v7x, 256 devices: a whole 4x4x8 slice. The times are simulated.
256 devices in a mesh: rows: 32 (over z_hi, y, core), rep: 8 (over z_lo, x).
Axes of the slice: x: 4, y: 4, z: 8 (z_hi: 4, z_lo: 2; z = z_hi * 2 + z_lo), core: 2. Of those that a mesh axis runs over, the one named last changes fastest.
Arguments:
- features: bfloat16 [32768, 256], P('rows'), may hold values from -6 to 6
- inv_sqrt_degree: bfloat16 [32768], P('rows'), may hold values from 0.25 to 1
- weight: bfloat16 [256, 256], replicated, may hold values from -0.375 to 0.375
- tile_vals: bfloat16 [32, 1024, 128, 128], P('rows', 'rep'), may hold values from -0.046875 to 0.046875
- tile_row: int32 [32, 1024], P('rows', 'rep'), may hold values from 0 to 7, as said below
- tile_col: int32 [32, 1024], P('rows', 'rep'), may hold values from 0 to 31, as said below
- tile_count: int32 [32, 32], P('rows', 'rep'), may hold values from 0 to 64, as said below
- cotangent: bfloat16 [32768, 256], P('rows'), may hold values from -6 to 6
Outputs:
- activated: bfloat16 [32768, 256], P(('rows', 'rep'))
- weight_grad: float32 [256, 256], replicated
- feature_grad: bfloat16 [32768, 256], P(('rep', 'rows'))
Inputs may be any that keep to these rules, and one draw needn't show every extreme that they name: `tile_count`: each count is at most 64; the 4 counts of row block i and columns r * 4 .. r * 4 + 3 sum to at most 128. Some pair holds exactly 64 tiles and some block row and replica exactly 128, in every draw. `tile_row`: the valid slots of a block row and replica are ordered by column block, and inside one block pair their positions are distinct. A valid slot counted for column block r * 4 + s has tile_col between s * 8 and s * 8 + 7.
All inputs are finite; a program needn't handle non-finite values.
Results may differ from a plain program's by a relative error of at most 0.015.
Values may be sent and summed in bfloat16 or wider, within the bound.
No kernel may reach another device: no remote copies, remote signals or barrier semaphores. Data moves between devices by JAX's collectives and lax.ppermute only.
A program may use at most 128 MiB of HBM per device.

v0:
```python
import jax
import jax.numpy as jnp
from jax import lax
from jax.sharding import PartitionSpec as P


def from_root(shard, axis, root):
    mine = lax.axis_index(axis) == root
    return lax.psum(jnp.where(mine, shard, jnp.zeros_like(shard)), axis)


def tile_products(values, out_index, in_index, keep, source, out_tiles, flipped):
    count = values.shape[0]
    block_size = 32
    turns = count // block_size
    width = source.shape[-1]
    tile = values.shape[-1]

    def advance(carry, block):
        vals_block, out_block, in_block, keep_block = block
        picked = source[in_block]
        if flipped:
            prod = jnp.einsum(
                "kji,kjf->kif", vals_block, picked, preferred_element_type=jnp.float32
            )
        else:
            prod = jnp.einsum(
                "kij,kjf->kif", vals_block, picked, preferred_element_type=jnp.float32
            )
        prod = jnp.where(keep_block[:, None, None], prod, jnp.float32(0.0))
        return (carry.at[out_block].add(prod), None)

    blocks = (
        values.reshape(turns, block_size, tile, tile),
        out_index.reshape(turns, block_size),
        in_index.reshape(turns, block_size),
        keep.reshape(turns, block_size),
    )
    initial = jnp.zeros((out_tiles, tile, width), jnp.float32)
    result, _ = lax.scan(advance, initial, blocks)
    return result


def section_window(values, out_rows, in_cols, starts, ends, section, per_block):
    slots = values.shape[0]
    pair_slots = per_block * per_block
    first = jnp.clip(starts[section], 0, slots - pair_slots)
    index = first + jnp.arange(pair_slots, dtype=jnp.int32)
    keep = (index >= starts[section]) & (index < ends[section])
    vals_window = lax.dynamic_slice_in_dim(values, first, pair_slots, 0)
    rows_window = lax.dynamic_slice_in_dim(out_rows, first, pair_slots, 0)
    cols_window = lax.dynamic_slice_in_dim(in_cols, first, pair_slots, 0)
    cols_window = jnp.clip(cols_window - section * per_block, 0, per_block - 1)
    return (vals_window, rows_window, cols_window, keep)


def shards(features, inv_sqrt_degree, weight, tile_vals, tile_row, tile_col, tile_count, cotangent):
    rows_count = lax.axis_size("rows")
    rep_count = lax.axis_size("rep")
    sections = rows_count // rep_count
    replica = lax.axis_index("rep")
    block_row = lax.axis_index("rows")
    nodes_block, width = features.shape
    tile = tile_vals.shape[-1]
    per_block = nodes_block // tile
    share = nodes_block // rep_count
    values = tile_vals[0]
    out_rows = tile_row[0]
    in_cols = tile_col[0]
    counts = tile_count[0]
    degree = inv_sqrt_degree.astype(jnp.float32)[:, None]
    scaled = (degree * features.astype(jnp.float32)).astype(jnp.bfloat16)
    ends = jnp.cumsum(counts)
    starts = ends - counts
    grad_factor = float(nodes_block * rows_count) ** (-0.5)
    arrived = []
    forward_sum = jnp.zeros((per_block, tile, width), jnp.float32)
    for section in range(sections):
        root = replica * sections + section
        block_feats, block_degree = (
            from_root(scaled, "rows", root),
            from_root(inv_sqrt_degree, "rows", root),
        )
        arrived.append((block_feats, block_degree))
        vals_window, rows_window, cols_window, keep = section_window(
            values, out_rows, in_cols, starts, ends, section, per_block
        )
        source = block_feats.reshape(per_block, tile, width)
        forward_sum = forward_sum + tile_products(
            vals_window, rows_window, cols_window, keep, source, per_block, False
        )
    partial_rows = forward_sum.reshape(nodes_block, width)
    summed = lax.psum(partial_rows, "rep")
    propagated = (degree * (summed + scaled.astype(jnp.float32))).astype(jnp.bfloat16)
    preact = jnp.dot(propagated, weight, preferred_element_type=jnp.float32)
    gate = jax.nn.sigmoid(preact)
    activated_block = (preact * gate).astype(jnp.bfloat16)
    grad_pre = (cotangent.astype(jnp.float32) * gate * (1.0 + preact * (1.0 - gate))).astype(
        jnp.bfloat16
    )
    back = (degree * jnp.dot(grad_pre, weight.T, preferred_element_type=jnp.float32)).astype(
        jnp.bfloat16
    )
    activated = lax.dynamic_slice_in_dim(activated_block, replica * share, share, 0)
    prop_share = lax.dynamic_slice_in_dim(propagated, replica * share, share, 0)
    grad_share = lax.dynamic_slice_in_dim(grad_pre, replica * share, share, 0)
    local_grad = lax.dot_general(
        prop_share, grad_share, (((0,), (0,)), ((), ())), preferred_element_type=jnp.float32
    )
    weight_grad = lax.psum(local_grad * grad_factor, ("rows", "rep"))
    back_tiles = back.reshape(per_block, tile, width)
    pieces = []
    for section in range(sections):
        vals_window, rows_window, cols_window, keep = section_window(
            values, out_rows, in_cols, starts, ends, section, per_block
        )
        pieces.append(
            tile_products(vals_window, cols_window, rows_window, keep, back_tiles, per_block, True)
        )
    terms = jnp.stack(pieces).reshape(sections, nodes_block, width)
    own_section = block_row - replica * sections
    section_ids = jnp.arange(sections, dtype=jnp.int32)
    self_part = jnp.where(
        (section_ids == own_section)[:, None, None],
        back.astype(jnp.float32)[None, :, :],
        jnp.float32(0.0),
    )
    degrees = jnp.stack([pair[1] for pair in arrived]).astype(jnp.float32)
    terms = (terms + self_part) * degrees[:, :, None]
    feature_grad = lax.psum_scatter(
        terms.reshape(sections * nodes_block, width), "rows", scatter_dimension=0, tiled=True
    ).astype(jnp.bfloat16)
    return (activated, weight_grad, feature_grad)


def solution(mesh):
    placed = (
        P("rows", None),
        P("rows"),
        P(),
        P("rows", "rep", None, None),
        P("rows", "rep"),
        P("rows", "rep"),
        P("rows", "rep"),
        P("rows", None),
    )
    return jax.shard_map(
        shards,
        mesh=mesh,
        in_specs=placed,
        out_specs=(P(("rows", "rep"), None), P(), P(("rep", "rows"), None)),
        check_vma=False,
    )
```

profile of v0, /device:TPU:2, one launch (start us, length us, event | category | flops | bytes accessed | tf_op | source)
XLA Modules:
  0.0 1060.3 jit_solution(3447704333140686903)
XLA Ops:
  8.0 2.7 broadcast_select_fusion.2
  20.7 9.3 constant_dynamic-slice_fusion.23
  30.0 276.2 %all-reduce.10.cloned.1.call-done = (bf16[8,128,256]{2,1,0:T(8,128)(2,1)}, bf16[8,128,256]{2,1,0:T(8,128)(2,1)}, bf16[8,128,256]{2,1,0:T(8,128)(2,1)}, bf16[8,128,256]{2,1,0:T(8,128)(2,1)}) async-done(((bf16[8,128,256]{2,1,0:T(8,128)(2,1)}, bf16[8,128,256]{2,1,0:T(8,128)(2,1)}, bf16[8,128,256]{2,1,0:T(8,128)(2,1)}, bf16[8,128,256]{2,1,0:T(8,128)(2,1)}), (bf16[8,128,256]{2,1,0:T(8,128)(2,1)}, ...) | async-done | bytes 2097168 | tf_op jit(solution)/shard_map/psum | solution.py:9
  306.3 28.3 %while.83 = (s32[]{:T(128)}, f32[8,128,256]{2,1,0:T(8,128)S(1)}, s32[2,32]{1,0:T(2,128)S(1)}, pred[2,32]{1,0:T(4,128)(4,1)S(1)}, bf16[2,32,128,128]{3,2,1,0:T(8,...) while((s32[]{:T(128)}, f32[8,128,256]{2,1,0:T(8,128)S(1)}, ...), condition=%wide.region_16.17_spmd, body=%wide.region_14.16_spmd.sunk | while | flops 270533824 | bytes 24122440 | solution.py:40
  306.4 3.1 gather_fusion.3
  309.5 4.5 convolution_select_fusion.19
  314.0 6.5 scatter_fusion.3
  320.5 3.1 gather_fusion.3
  323.6 4.5 convolution_select_fusion.19
  328.2 6.5 scatter_fusion.3
  334.7 26.2 %while.82 = (s32[]{:T(128)}, f32[8,128,256]{2,1,0:T(8,128)S(1)}, s32[2,32]{1,0:T(2,128)S(1)}, pred[2,32]{1,0:T(4,128)(4,1)S(1)}, bf16[2,32,128,128]{3,2,1,0:T(8,...) while((s32[]{:T(128)}, f32[8,128,256]{2,1,0:T(8,128)S(1)}, ...), condition=%wide.region_12.13_spmd, body=%wide.region_10.12_spmd.sunk | while | flops 270533824 | bytes 24122440 | solution.py:40
  334.8 2.0 gather_fusion.2
  336.8 4.5 convolution_select_fusion.18
  341.4 6.5 scatter_fusion.2
  347.9 2.0 gather_fusion.2
  349.9 4.5 convolution_select_fusion.18
  354.5 6.5 scatter_fusion.2
  361.0 28.3 %while.80 = (s32[]{:T(128)}, f32[8,128,256]{2,1,0:T(8,128)S(1)}, s32[2,32]{1,0:T(2,128)S(1)}, pred[2,32]{1,0:T(4,128)(4,1)S(1)}, bf16[2,32,128,128]{3,2,1,0:T(8,...) while((s32[]{:T(128)}, f32[8,128,256]{2,1,0:T(8,128)S(1)}, ...), condition=%wide.region_4.5_spmd, body=%wide.region_2.4_spmd.sunk | while | flops 270533824 | bytes 24122440 | solution.py:40
  361.1 3.1 gather_fusion
  364.2 4.5 convolution_select_fusion.16
  368.7 6.5 scatter_fusion
  375.2 3.1 gather_fusion
  378.3 4.5 convolution_select_fusion.16
  382.9 6.5 scatter_fusion
  390.4 34.4 %while.81 = (s32[]{:T(128)}, f32[8,128,256]{2,1,0:T(8,128)}, s32[2,32]{1,0:T(2,128)S(1)}, pred[2,32]{1,0:T(4,128)(4,1)S(1)}, bf16[2,32,128,128]{3,2,1,0:T(8,128)...) while((s32[]{:T(128)}, f32[8,128,256]{2,1,0:T(8,128)}, s32[2,32]{1,0:T(2,128)S(1)}, ...), condition=%wide.region_8.9_spmd, body=%wide.region_6.8_spmd.sunk | while | flops 270533824 | bytes 24122440 | solution.py:40
  390.4 3.1 gather_fusion.1
  393.5 4.5 convolution_select_fusion.17
  398.1 9.6 scatter_fusion.1
  407.7 3.1 gather_fusion.1
  410.8 4.5 convolution_select_fusion.17
  415.3 9.5 scatter_fusion.1
  424.8 2.5 add_add_fusion
  427.3 4.2 copy.25
  431.6 2.9 copy.23
  434.5 4.2 copy.21
  438.7 2.9 copy.19
  441.7 144.0 %all-reduce = (bf16[1,1024,1]{1,2,0:T(2,128)(2,1)S(1)}, bf16[1,1024,1]{1,2,0:T(2,128)(2,1)S(1)}, bf16[1,1024,1]{1,2,0:T(2,128)(2,1)S(1)}, bf16[1,1024,1]{1,2,0:T(2,128)(2,1)S(1)}) all-reduce(bf16[1,1024,1]{1,2,0:T(2,128)(2,1)S(1)} %stack.41, bf16[1,1024,1]{1,2,0:T(2,128)(2,1)S(1)} %stack.40, ...), channel_id=1, replica_groups=mesh['rows'=32,'rep'=8] {'rows'}, use_global_device_ids=true, to_apply=%region_34.35 | all-reduce | flops 4096 | bytes 16384 | tf_op jit(solution)/shard_map/psum | solution.py:9
  590.5 26.1 %while.87 = (s32[]{:T(128)}, f32[8,128,256]{2,1,0:T(8,128)S(1)}, s32[2,32]{1,0:T(2,128)S(1)}, pred[2,32]{1,0:T(4,128)(4,1)S(1)}, bf16[2,32,128,128]{2,3,1,0:T(8,...) while((s32[]{:T(128)}, f32[8,128,256]{2,1,0:T(8,128)S(1)}, ...), condition=%wide.region_30.31_spmd, body=%wide.region_28.30_spmd.sunk | while | flops 270533824 | bytes 24122440 | solution.py:40
  590.6 2.0 gather_fusion.7
  592.6 4.5 convolution_select_fusion.23
  597.1 6.5 scatter_fusion.7
  603.6 2.0 gather_fusion.7
  605.7 4.5 convolution_select_fusion.23
  610.2 6.4 scatter_fusion.7
  616.8 26.1 %while.86 = (s32[]{:T(128)}, f32[8,128,256]{2,1,0:T(8,128)S(1)}, s32[2,32]{1,0:T(2,128)S(1)}, pred[2,32]{1,0:T(4,128)(4,1)S(1)}, bf16[2,32,128,128]{2,3,1,0:T(8,...) while((s32[]{:T(128)}, f32[8,128,256]{2,1,0:T(8,128)S(1)}, ...), condition=%wide.region_27.28_spmd, body=%wide.region_25.27_spmd.sunk | while | flops 270533824 | bytes 24122440 | solution.py:40
  616.8 2.0 gather_fusion.6
  618.8 4.5 convolution_select_fusion.22
  623.4 6.4 scatter_fusion.6
  629.8 2.0 gather_fusion.6
  631.9 4.5 convolution_select_fusion.22
  636.4 6.4 scatter_fusion.6
  644.1 28.1 %while.85 = (s32[]{:T(128)}, f32[8,128,256]{2,1,0:T(8,128)}, s32[2,32]{1,0:T(2,128)S(1)}, pred[2,32]{1,0:T(4,128)(4,1)S(1)}, bf16[2,32,128,128]{2,3,1,0:T(8,128)...) while((s32[]{:T(128)}, f32[8,128,256]{2,1,0:T(8,128)}, ...), condition=%wide.region_24.25_spmd, body=%wide.region_22.24_spmd.sunk | while | flops 270533824 | bytes 32511104 | solution.py:40
  646.2 4.6 convolution_select_fusion.21
  650.8 6.4 scatter_fusion.5
  660.2 4.6 convolution_select_fusion.21
  664.8 6.4 scatter_fusion.5
  672.3 26.1 %while.84 = (s32[]{:T(128)}, f32[8,128,256]{2,1,0:T(8,128)S(1)}, s32[2,32]{1,0:T(2,128)S(1)}, pred[2,32]{1,0:T(4,128)(4,1)S(1)}, bf16[2,32,128,128]{2,3,1,0:T(8,...) while((s32[]{:T(128)}, f32[8,128,256]{2,1,0:T(8,128)S(1)}, ...), condition=%wide.region_21.22_spmd, body=%wide.region_19.21_spmd.sunk | while | flops 270533824 | bytes 24122440 | solution.py:40
  674.4 4.5 convolution_select_fusion.20
  679.0 6.4 scatter_fusion.4
  687.5 4.5 convolution_select_fusion.20
  692.0 6.4 scatter_fusion.4
  700.5 2.8 fusion.57
  706.8 91.9 %reduce-scatter.2.cloned.1.call-done = f32[128,256]{1,0:T(8,128)} async-done(((f32[4096,256]{1,0:T(8,128)}), f32[128,256]{1,0:T(8,128)}) %reduce-scatter.2.cloned.1.call-update) | async-done | bytes 131088 | tf_op jit(solution)/shard_map/reduce_scatter | solution.py:130
  800.3 251.8 %all-reduce.8.cloned.1.call-done = f32[256,256]{1,0:T(8,128)} async-done(((f32[256,256]{1,0:T(8,128)}), f32[256,256]{1,0:T(8,128)}) %all-reduce.8.cloned.1.call-update) | async-done | bytes 262160 | tf_op jit(solution)/shard_map/psum | solution.py:110
  (141 shorter events, 34.9 us)
Async XLA Ops:
  7.2 580.1 %copy-start = (bf16[256,256]{1,0:T(8,128)(2,1)S(1)}, bf16[256,256]{1,0:T(8,128)(2,1)}, u32[]{:S(2)}) copy-start(bf16[256,256]{1,0:T(8,128)(2,1)} %param.26) | copy-start | bytes 393220
  7.2 299.0 %all-reduce.10.cloned.1.call-start = ((), (), s32[]{:S(2)}) async-start(), calls=%async_computation.4 | async-start | bytes 4194304 | tf_op jit(solution)/shard_map/psum | solution.py:9
  8.0 2.8 copy-start.16
  8.0 6.2 copy-start.11
  8.0 6.2 copy-start.12
  10.7 575.1 %all-reduce.6.cloned.1.call-start = ((), (), s32[]{:S(2)}) async-start(), calls=%async_computation.1 | async-start | bytes 2097152 | tf_op jit(solution)/shard_map/psum | solution.py:93
  306.3 28.4 %copy-start.5 = (bf16[8,128,256]{2,1,0:T(8,128)(2,1)S(1)}, bf16[8,128,256]{2,1,0:T(8,128)(2,1)}, u32[]{:S(2)}) copy-start(bf16[8,128,256]{2,1,0:T(8,128)(2,1)} %get-tuple-element.943) | copy-start | bytes 1572868
  389.3 1.1 copy-start.13
  427.3 371.4 %reduce-scatter.2.cloned.1.call-start = ((), (), s32[]{:S(2)}) async-start(), calls=%async_computation.3 | async-start | bytes 4325376 | tf_op jit(solution)/shard_map/reduce_scatter | solution.py:130
  427.3 4.2 copy-start.7
  434.5 4.2 copy-start.6
  438.7 147.1 %copy-start.9 = (bf16[1024,256]{1,0:T(8,128)(2,1)S(1)}, bf16[1024,256]{1,0:T(8,128)(2,1)}, u32[]{:S(2)}) copy-start(bf16[1024,256]{1,0:T(8,128)(2,1)} %param.24) | copy-start | bytes 1572868
  441.6 145.7 %copy-start.15 = (bf16[1024,256]{1,0:T(8,128)(2,1)S(1)}, bf16[1024,256]{1,0:T(8,128)(2,1)}, u32[]{:S(2)}) copy-start(bf16[1024,256]{1,0:T(8,128)(2,1)} %param.31) | copy-start | bytes 1572868
  587.3 1.8 copy-start.10
  642.8 1.3 copy-start.2
  644.0 28.3 %copy-start.14 = (pred[2,32]{1,0:T(4,128)(4,1)S(1)}, pred[2,32]{1,0:T(4,128)(4,1)}, u32[]{:S(2)}) copy-start(pred[2,32]{1,0:T(4,128)(4,1)} %copy-done.13) | copy-start | bytes 196
  646.2 4.6 copy-start.3
  657.2 1.0 copy-start.4
  660.2 4.6 copy-start.3
  671.3 1.0 copy-start.4
  698.4 2.0 copy-start.8
  703.3 350.4 %copy-start.1 = (bf16[256,256]{1,0:T(8,128)(2,1)S(1)}, bf16[256,256]{1,0:T(8,128)(2,1)}, u32[]{:S(2)}) copy-start(bf16[256,256]{1,0:T(8,128)(2,1)} %param.26) | copy-start | bytes 393220
  703.4 348.7 %all-reduce.8.cloned.1.call-start = ((), (), s32[]{:S(2)}) async-start(), calls=%async_computation.2 | async-start | bytes 524288 | tf_op jit(solution)/shard_map/psum | solution.py:110
Sparse Core Ops, SparseCore 0:
  10.9 295.2 all-reduce.9
  427.4 79.0 all-reduce.5
  703.5 95.2 reduce-scatter.1
  804.6 247.4 all-reduce.7
where the time goes:
time: 1060 us
  waiting for transfers between devices  620 us (58%)
  blocking collectives  144 us (14%)
  other arithmetic  130 us (12%)
  matrix products  77.7 us (7%)
  local copies, waits for them, and re-layouts  71.1 us (7%)
  between operations  16.7 us (2%)
    psum x1, waiting for transfers between devices, from_root(): return lax.psum(jnp.where(mine, shard, jnp.zeros_like(shard)), axis)  276 us
    psum x1, waiting for transfers between devices, shards(): weight_grad = lax.psum(local_grad * grad_factor, ('rows', 'rep'))  252 us
    psum x1, blocking collectives, from_root(): return lax.psum(jnp.where(mine, shard, jnp.zeros_like(shard)), axis)  144 us
    scatter-add x16, other arithmetic, advance(): return (carry.at[out_block].add(prod), None)  109 us
    reduce_scatter x1, waiting for transfers between devices, shards(): lax.psum_scatter(terms.reshape(sections * nodes_block, width), 'rows', sc...  91.9 us
    gather x16, local copies, waits for them, and re-layouts, advance(): picked = source[in_block]  38.8 us
    dot_general x8, matrix products, advance(): jnp.einsum('kji,kjf->kif', vals_block, picked, preferred_element_type=jnp...  36.5 us
    dot_general x8, matrix products, advance(): jnp.einsum('kij,kjf->kif', vals_block, picked, preferred_element_type=jnp...  36.3 us
  transfers between devices with their start and end apart: 4, of which 3 were waited for; matrix products, arithmetic and copies ran while one was open for 3% of the time, Pallas kernels for 0%

commit v1 on v0

--- a/solution.py
+++ b/solution.py
@@ -4,9 +4,15 @@
 from jax.sharding import PartitionSpec as P
 
 
+def add_all(x, mesh_axis):
+    shards = lax.all_gather(x, mesh_axis, axis=0, tiled=False)
+    total = shards.sum(axis=0)
+    return total
+
+
 def from_root(shard, axis, root):
     mine = lax.axis_index(axis) == root
-    return lax.psum(jnp.where(mine, shard, jnp.zeros_like(shard)), axis)
+    return add_all(jnp.where(mine, shard, jnp.zeros_like(shard)), axis)
 
 
 def tile_products(values, out_index, in_index, keep, source, out_tiles, flipped):

time: 1060 us -> 1280 us (1.21)
  waiting for transfers between devices: 620 us -> 770 us
  other arithmetic: 130 us -> 176 us
  blocking collectives: 144 us -> 173 us
    all_gather x0 -> x4, waiting for transfers between devices: none -> 421 us  [add_all(): shards = lax.all_gather(x, mesh_axis, axis=0, tiled=False)]
    psum x1 -> x0, waiting for transfers between devices: 276 us -> none  [from_root(): return lax.psum(jnp.where(mine, shard, jnp.zeros_like(shard)), axis)]
    all_gather x0 -> x4, blocking collectives: none -> 173 us  [add_all(): shards = lax.all_gather(x, mesh_axis, axis=0, tiled=False)]
    psum x1 -> x0, blocking collectives: 144 us -> none  [from_root(): return lax.psum(jnp.where(mine, shard, jnp.zeros_like(shard)), axis)]
    reduce_sum x0 -> x8, other arithmetic: none -> 36.8 us  [add_all(): total = shards.sum(axis=0)]
  transfers between devices with their start and end apart: 4 -> 7, of which waited for: 3 -> 6; matrix products, arithmetic and copies ran while one was open for 3% -> 5% of each run, Pallas kernels for 0% -> 0%
where the time goes in v1:
time: 1280 us
  waiting for transfers between devices  770 us (60%)
  other arithmetic  176 us (14%)
  blocking collectives  173 us (14%)
  matrix products  77.5 us (6%)
  local copies, waits for them, and re-layouts  67.7 us (5%)
  between operations  17 us (1%)
    all_gather x4, waiting for transfers between devices, add_all(): shards = lax.all_gather(x, mesh_axis, axis=0, tiled=False)  421 us
    psum x1, waiting for transfers between devices, shards(): weight_grad = lax.psum(local_grad * grad_factor, ('rows', 'rep'))  253 us
    all_gather x4, blocking collectives, add_all(): shards = lax.all_gather(x, mesh_axis, axis=0, tiled=False)  173 us
    scatter-add x16, other arithmetic, advance(): return (carry.at[out_block].add(prod), None)  118 us
    reduce_scatter x1, waiting for transfers between devices, shards(): lax.psum_scatter(terms.reshape(sections * nodes_block, width), 'rows', sc...  94.2 us
    reduce_sum x8, other arithmetic, add_all(): total = shards.sum(axis=0)  36.8 us
    gather x16, local copies, waits for them, and re-layouts, advance(): picked = source[in_block]  36.5 us
    dot_general x8, matrix products, advance(): jnp.einsum('kij,kjf->kif', vals_block, picked, preferred_element_type=jnp...  36.3 us
  transfers between devices with their start and end apart: 7, of which 6 were waited for; matrix products, arithmetic and copies ran while one was open for 5% of the time, Pallas kernels for 0%

profile of v1, /device:TPU:2, one launch (start us, length us, event | category | flops | bytes accessed | tf_op | source)
XLA Modules:
  0.0 1281.8 jit_solution(440973740810585515)
XLA Ops:
  23.9 9.1 constant_dynamic-slice_fusion.23
  33.0 90.5 %all-gather.15.cloned.1.call-done = bf16[32768,256]{1,0:T(8,128)(2,1)} async-done(((bf16[1024,256]{1,0:T(8,128)(2,1)}), bf16[32768,256]{1,0:T(8,128)(2,1)}) %all-gather.15.cloned.1.call-update) | async-done | bytes 16777232 | tf_op jit(solution)/shard_map/all_gather | solution.py:8
  123.5 9.7 reduce_sum.97
  133.2 109.4 %all-gather.17.cloned.1.call-done = bf16[32768,256]{1,0:T(8,128)(2,1)} async-done(((bf16[1024,256]{1,0:T(8,128)(2,1)}), bf16[32768,256]{1,0:T(8,128)(2,1)}) %all-gather.17.cloned.1.call-update) | async-done | bytes 16777232 | tf_op jit(solution)/shard_map/all_gather | solution.py:8
  242.6 8.7 reduce_sum.98
  251.4 110.5 %all-gather.19.cloned.1.call-done = bf16[32768,256]{1,0:T(8,128)(2,1)} async-done(((bf16[1024,256]{1,0:T(8,128)(2,1)}), bf16[32768,256]{1,0:T(8,128)(2,1)}) %all-gather.19.cloned.1.call-update) | async-done | bytes 16777232 | tf_op jit(solution)/shard_map/all_gather | solution.py:8
  361.8 8.7 reduce_sum.99
  370.6 110.2 %all-gather.13.cloned.1.call-done = bf16[32768,256]{1,0:T(8,128)(2,1)} async-done(((bf16[1024,256]{1,0:T(8,128)(2,1)}), bf16[32768,256]{1,0:T(8,128)(2,1)}) %all-gather.13.cloned.1.call-update) | async-done | bytes 16777232 | tf_op jit(solution)/shard_map/all_gather | solution.py:8
  480.8 9.5 reduce_sum.96
  490.4 26.2 %while.82 = (s32[]{:T(128)}, f32[8,128,256]{2,1,0:T(8,128)S(1)}, s32[2,32]{1,0:T(2,128)S(1)}, pred[2,32]{1,0:T(4,128)(4,1)S(1)}, bf16[2,32,128,128]{3,2,1,0:T(8,...) while((s32[]{:T(128)}, f32[8,128,256]{2,1,0:T(8,128)S(1)}, ...), condition=%wide.region_12.13_spmd, body=%wide.region_10.12_spmd.sunk | while | flops 270533824 | bytes 24122440 | solution.py:46
  492.5 4.5 convolution_select_fusion.18
  497.0 6.5 scatter_fusion.2
  505.6 4.5 convolution_select_fusion.18
  510.1 6.5 scatter_fusion.2
  516.7 26.2 %while.83 = (s32[]{:T(128)}, f32[8,128,256]{2,1,0:T(8,128)S(1)}, s32[2,32]{1,0:T(2,128)S(1)}, pred[2,32]{1,0:T(4,128)(4,1)S(1)}, bf16[2,32,128,128]{3,2,1,0:T(8,...) while((s32[]{:T(128)}, f32[8,128,256]{2,1,0:T(8,128)S(1)}, ...), condition=%wide.region_16.17_spmd, body=%wide.region_14.16_spmd.sunk | while | flops 270533824 | bytes 24122440 | solution.py:46
  518.7 4.5 convolution_select_fusion.19
  523.3 6.5 scatter_fusion.3
  531.8 4.5 convolution_select_fusion.19
  536.4 6.5 scatter_fusion.3
  542.9 28.3 %while.80 = (s32[]{:T(128)}, f32[8,128,256]{2,1,0:T(8,128)S(1)}, s32[2,32]{1,0:T(2,128)S(1)}, pred[2,32]{1,0:T(4,128)(4,1)S(1)}, bf16[2,32,128,128]{3,2,1,0:T(8,...) while((s32[]{:T(128)}, f32[8,128,256]{2,1,0:T(8,128)S(1)}, ...), condition=%wide.region_4.5_spmd, body=%wide.region_2.4_spmd.sunk | while | flops 270533824 | bytes 24122440 | solution.py:46
  543.0 3.1 gather_fusion
  546.0 4.5 convolution_select_fusion.16
  550.6 6.5 scatter_fusion
  557.1 3.1 gather_fusion
  560.2 4.5 convolution_select_fusion.16
  564.7 6.5 scatter_fusion
  572.3 34.8 %while.81 = (s32[]{:T(128)}, f32[8,128,256]{2,1,0:T(8,128)}, s32[2,32]{1,0:T(2,128)S(1)}, pred[2,32]{1,0:T(4,128)(4,1)S(1)}, bf16[2,32,128,128]{3,2,1,0:T(8,128)...) while((s32[]{:T(128)}, f32[8,128,256]{2,1,0:T(8,128)}, s32[2,32]{1,0:T(2,128)S(1)}, ...), condition=%wide.region_8.9_spmd, body=%wide.region_6.8_spmd.sunk | while | flops 270533824 | bytes 24122440 | solution.py:46
  572.3 3.1 gather_fusion.1
  575.4 4.5 convolution_select_fusion.17
  579.9 9.8 scatter_fusion.1
  589.7 3.1 gather_fusion.1
  592.7 4.5 convolution_select_fusion.17
  597.3 9.8 scatter_fusion.1
  609.7 4.4 copy.37
  614.1 2.9 copy.35
  617.0 4.2 copy.41
  621.3 3.0 copy.39
  624.3 53.5 %all-gather.4 = bf16[32768]{0:T(1024)(128)(2,1)S(1)} all-gather(bf16[1024]{0:T(1024)(128)(2,1)S(1)} %copy-done.15), channel_id=6, replica_groups=mesh['rows'=32,'rep'=8] {'rows'}, dimensions={0}, use_global_device_ids=true | all-gather | bytes 67584 | tf_op jit(solution)/shard_map/all_gather | solution.py:8
  677.9 39.3 %all-gather.5 = bf16[32768]{0:T(1024)(128)(2,1)S(1)} all-gather(bf16[1024]{0:T(1024)(128)(2,1)S(1)} %copy-done.14), channel_id=7, replica_groups=mesh['rows'=32,'rep'=8] {'rows'}, dimensions={0}, use_global_device_ids=true | all-gather | bytes 67584 | tf_op jit(solution)/shard_map/all_gather | solution.py:8
  717.3 40.7 %all-gather.7 = bf16[32768]{0:T(1024)(128)(2,1)S(1)} all-gather(bf16[1024]{0:T(1024)(128)(2,1)S(1)} %copy-done.13), channel_id=9, replica_groups=mesh['rows'=32,'rep'=8] {'rows'}, dimensions={0}, use_global_device_ids=true | all-gather | bytes 67584 | tf_op jit(solution)/shard_map/all_gather | solution.py:8
  758.0 39.3 %all-gather.6 = bf16[32768]{0:T(1024)(128)(2,1)S(1)} all-gather(bf16[1024]{0:T(1024)(128)(2,1)S(1)} %copy-done.12), channel_id=8, replica_groups=mesh['rows'=32,'rep'=8] {'rows'}, dimensions={0}, use_global_device_ids=true | all-gather | bytes 67584 | tf_op jit(solution)/shard_map/all_gather | solution.py:8
  802.2 26.2 %while.87 = (s32[]{:T(128)}, f32[8,128,256]{2,1,0:T(8,128)S(1)}, s32[2,32]{1,0:T(2,128)S(1)}, pred[2,32]{1,0:T(4,128)(4,1)S(1)}, bf16[2,32,128,128]{2,3,1,0:T(8,...) while((s32[]{:T(128)}, f32[8,128,256]{2,1,0:T(8,128)S(1)}, ...), condition=%wide.region_30.31_spmd, body=%wide.region_28.30_spmd.sunk | while | flops 270533824 | bytes 24122440 | solution.py:46
  804.3 4.5 convolution_select_fusion.23
  808.9 6.5 scatter_fusion.7
  817.4 4.5 convolution_select_fusion.23
  822.0 6.4 scatter_fusion.7
  828.5 26.0 %while.86 = (s32[]{:T(128)}, f32[8,128,256]{2,1,0:T(8,128)S(1)}, s32[2,32]{1,0:T(2,128)S(1)}, pred[2,32]{1,0:T(4,128)(4,1)S(1)}, bf16[2,32,128,128]{2,3,1,0:T(8,...) while((s32[]{:T(128)}, f32[8,128,256]{2,1,0:T(8,128)S(1)}, ...), condition=%wide.region_27.28_spmd, body=%wide.region_25.27_spmd.sunk | while | flops 270533824 | bytes 24122440 | solution.py:46
  830.5 4.5 convolution_select_fusion.22
  835.1 6.4 scatter_fusion.6
  843.5 4.5 convolution_select_fusion.22
  848.1 6.4 scatter_fusion.6
  855.8 34.2 %while.85 = (s32[]{:T(128)}, f32[8,128,256]{2,1,0:T(8,128)}, s32[2,32]{1,0:T(2,128)S(1)}, pred[2,32]{1,0:T(4,128)(4,1)S(1)}, bf16[2,32,128,128]{2,3,1,0:T(8,128)...) while((s32[]{:T(128)}, f32[8,128,256]{2,1,0:T(8,128)}, ...), condition=%wide.region_24.25_spmd, body=%wide.region_22.24_spmd.sunk | while | flops 270533824 | bytes 24122440 | solution.py:46
  857.9 4.5 convolution_select_fusion.21
  862.4 11.1 scatter_fusion.5
  875.7 4.5 convolution_select_fusion.21
  880.2 9.8 scatter_fusion.5
  890.1 26.1 %while.84 = (s32[]{:T(128)}, f32[8,128,256]{2,1,0:T(8,128)S(1)}, s32[2,32]{1,0:T(2,128)S(1)}, pred[2,32]{1,0:T(4,128)(4,1)S(1)}, bf16[2,32,128,128]{2,3,1,0:T(8,...) while((s32[]{:T(128)}, f32[8,128,256]{2,1,0:T(8,128)S(1)}, ...), condition=%wide.region_21.22_spmd, body=%wide.region_19.21_spmd.sunk | while | flops 270533824 | bytes 24122440 | solution.py:46
  892.2 4.5 convolution_select_fusion.20
  896.7 6.4 scatter_fusion.4
  905.3 4.5 convolution_select_fusion.20
  909.8 6.4 scatter_fusion.4
  918.3 2.8 fusion.57
  924.6 94.2 %reduce-scatter.2.cloned.1.call-done = f32[128,256]{1,0:T(8,128)} async-done(((f32[4096,256]{1,0:T(8,128)}), f32[128,256]{1,0:T(8,128)}) %reduce-scatter.2.cloned.1.call-update) | async-done | bytes 131088 | tf_op jit(solution)/shard_map/reduce_scatter | solution.py:136
  1020.4 252.9 %all-reduce.5.cloned.1.call-done = f32[256,256]{1,0:T(8,128)} async-done(((f32[256,256]{1,0:T(8,128)}), f32[256,256]{1,0:T(8,128)}) %all-reduce.5.cloned.1.call-update) | async-done | bytes 262160 | tf_op jit(solution)/shard_map/psum | solution.py:116
  (163 shorter events, 57.9 us)
Async XLA Ops:
  7.2 791.8 %copy-start = (bf16[256,256]{1,0:T(8,128)(2,1)S(1)}, bf16[256,256]{1,0:T(8,128)(2,1)}, u32[]{:S(2)}) copy-start(bf16[256,256]{1,0:T(8,128)(2,1)} %param.26) | copy-start | bytes 393220
  7.2 116.3 %all-gather.15.cloned.1.call-start = ((), (), s32[]{:S(2)}) async-start(), calls=%async_computation.5 | async-start | bytes 17301504 | tf_op jit(solution)/shard_map/all_gather | solution.py:8
  8.6 0.6 copy-start.8
  9.2 4.8 copy-start.17
  9.2 8.2 copy-start.10
  9.2 8.2 copy-start.11
  11.9 230.7 %all-gather.17.cloned.1.call-start = ((), (), s32[]{:S(2)}) async-start(), calls=%async_computation.6 | async-start | bytes 17301504 | tf_op jit(solution)/shard_map/all_gather | solution.py:8
  12.7 349.2 %all-gather.19.cloned.1.call-start = ((), (), s32[]{:S(2)}) async-start(), calls=%async_computation.7 | async-start | bytes 17301504 | tf_op jit(solution)/shard_map/all_gather | solution.py:8
  13.4 467.4 %all-gather.13.cloned.1.call-start = ((), (), s32[]{:S(2)}) async-start(), calls=%async_computation.4 | async-start | bytes 17301504 | tf_op jit(solution)/shard_map/all_gather | solution.py:8
  14.0 783.5 %all-reduce.3.cloned.1.call-start = ((), (), s32[]{:S(2)}) async-start(), calls=%async_computation.1 | async-start | bytes 2097152 | tf_op jit(solution)/shard_map/psum | solution.py:99
  609.6 409.2 %reduce-scatter.2.cloned.1.call-start = ((), (), s32[]{:S(2)}) async-start(), calls=%async_computation.3 | async-start | bytes 4325376 | tf_op jit(solution)/shard_map/reduce_scatter | solution.py:136
  609.7 4.4 copy-start.4
  617.0 4.2 copy-start.3
  621.2 3.1 copy-start.15
  621.2 56.7 %copy-start.14 = (bf16[1024]{0:T(1024)(128)(2,1)S(1)}, bf16[1024]{0:T(1024)(128)(2,1)}, u32[]{:S(2)}) copy-start(bf16[1024]{0:T(1024)(128)(2,1)} %get-tuple-element.566) | copy-start | bytes 6148
  621.2 96.1 %copy-start.13 = (bf16[1024]{0:T(1024)(128)(2,1)S(1)}, bf16[1024]{0:T(1024)(128)(2,1)}, u32[]{:S(2)}) copy-start(bf16[1024]{0:T(1024)(128)(2,1)} %get-tuple-element.568) | copy-start | bytes 6148
  621.2 136.8 %copy-start.12 = (bf16[1024]{0:T(1024)(128)(2,1)S(1)}, bf16[1024]{0:T(1024)(128)(2,1)}, u32[]{:S(2)}) copy-start(bf16[1024]{0:T(1024)(128)(2,1)} %get-tuple-element.569) | copy-start | bytes 6148
  621.3 176.2 %copy-start.6 = (bf16[1024,256]{1,0:T(8,128)(2,1)S(1)}, bf16[1024,256]{1,0:T(8,128)(2,1)}, u32[]{:S(2)}) copy-start(bf16[1024,256]{1,0:T(8,128)(2,1)} %param.24) | copy-start | bytes 1572868
  621.3 176.2 %copy-start.9 = (f32[1024]{0:T(1024)S(1)}, f32[1024]{0:T(1024)}, u32[]{:S(2)}) copy-start(f32[1024]{0:T(1024)} %copy-done.8) | copy-start | bytes 12292
  624.2 174.8 %copy-start.16 = (bf16[1024,256]{1,0:T(8,128)(2,1)S(1)}, bf16[1024,256]{1,0:T(8,128)(2,1)}, u32[]{:S(2)}) copy-start(bf16[1024,256]{1,0:T(8,128)(2,1)} %param.31) | copy-start | bytes 1572868
  799.0 1.8 copy-start.7
  854.5 1.3 copy-start.2
  916.2 2.0 copy-start.5
  921.1 353.8 %copy-start.1 = (bf16[256,256]{1,0:T(8,128)(2,1)S(1)}, bf16[256,256]{1,0:T(8,128)(2,1)}, u32[]{:S(2)}) copy-start(bf16[256,256]{1,0:T(8,128)(2,1)} %param.26) | copy-start | bytes 393220
  921.1 352.1 %all-reduce.5.cloned.1.call-start = ((), (), s32[]{:S(2)}) async-start(), calls=%async_computation.2 | async-start | bytes 524288 | tf_op jit(solution)/shard_map/psum | solution.py:116
Sparse Core Ops, SparseCore 0:
  12.0 111.3 all-gather.14
  126.0 116.5 all-gather.16
  245.2 116.5 all-gather.18
  364.2 116.5 all-gather.12
  609.7 88.0 all-reduce.2
  921.3 97.5 reduce-scatter.1
  1025.7 247.4 all-reduce.4
